TPU v7x, 512 devices: a whole 4x4x16 slice. The times are simulated.
512 devices in a mesh: dp: 2 (over core), ctx: 64 (over x, z), head: 4 (over y).
Axes of the slice: x: 4, y: 4, z: 16, core: 2. Of those that a mesh axis runs over, the one named last changes fastest.
Arguments:
- query: bfloat16 [2, 64, 4, 512, 256], P('dp', 'ctx', 'head'), may hold values from -120 to 120
- key: bfloat16 [2, 8192, 4096], P('dp', 'ctx', 'head'), may hold values from -8 to 8
- value: bfloat16 [2, 8192, 4096], P('dp', 'ctx', 'head'), may hold values from -6 to 6
- grad_out: bfloat16 [2, 64, 4, 512, 256], P('dp', 'ctx', 'head'), may hold values from -6 to 6
- chosen: int32 [2, 16, 32, 3], P('dp', None, 'head'), may hold values from 0 to 15, as said below
- placed: int32 [16], replicated, may hold values from 0 to 15, each once
- sink: float32 [32], P('head'), may hold values from -2 to 6
Outputs:
- attended: bfloat16 [2, 64, 4, 512, 256], P('dp', 'ctx', 'head')
- grad_query: bfloat16 [2, 64, 4, 512, 256], P('dp', 'ctx', 'head')
- grad_key: bfloat16 [2, 8192, 4096], P('dp', 'ctx', 'head')
- grad_value: bfloat16 [2, 8192, 4096], P('dp', 'ctx', 'head')
- grad_sink: float32 [32], replicated
Inputs may be any that keep to these rules, and one draw needn't show every extreme that they name: `chosen`: for each sequence, block b and head, the first min(b, 3) entries are distinct blocks before b; the remaining entries are blocks from b to 15. `placed`: every block is held by exactly one slot.
All inputs are finite; a program needn't handle non-finite values.
Results may differ from a plain program's by a relative error of at most 0.025.
Values may be sent and summed in bfloat16 or wider, within the bound.
No kernel may reach another device: no remote copies, remote signals or barrier semaphores. Data moves between devices by JAX's collectives and lax.ppermute only.
A program may use at most 64 MiB of HBM per device.

v0:
```python
import math
import jax
import jax.numpy as jnp
from jax import lax
from jax.sharding import PartitionSpec as P

HEADS = 32
DH = 128


def inner_rows(left, right):
    return lax.dot_general(
        left, right, (((1,), (1,)), ((), ())), preferred_element_type=jnp.float32
    )


def outer_rows(left, right):
    return lax.dot_general(
        left, right, (((0,), (0,)), ((), ())), preferred_element_type=jnp.float32
    )


def attend_block(query_rows, grad_rows, tiles, usable, sink_logit):
    rows, width = query_rows.shape
    scale = 1.0 / math.sqrt(width)
    keys = tiles[:, :, :width].reshape(-1, width)
    vals = tiles[:, :, width:].reshape(-1, width)
    scores = inner_rows(query_rows, keys) * scale
    cols = tiles.shape[0] * rows
    tile_of = jnp.arange(cols) // rows
    offset = jnp.arange(cols) % rows
    own_ok = offset[None, :] <= jnp.arange(rows)[:, None]
    allowed = jnp.where(tile_of[None, :] == 0, own_ok, usable[tile_of][None, :])
    masked = jnp.where(allowed, scores, -jnp.inf)
    top = jnp.maximum(jnp.max(masked, axis=1), sink_logit)
    expo = jnp.exp(masked - top[:, None])
    sink_part = jnp.exp(sink_logit - top)
    total = sink_part + jnp.sum(expo, axis=1)
    prob = expo / total[:, None]
    weights = prob.astype(jnp.bfloat16)
    attended = jnp.dot(weights, vals, preferred_element_type=jnp.float32).astype(jnp.bfloat16)
    stored = lax.optimization_barrier(attended)
    delta = jnp.sum(grad_rows.astype(jnp.float32) * stored.astype(jnp.float32), axis=1)
    dprob = inner_rows(grad_rows, vals)
    dscore = (prob * (dprob - delta[:, None]) * scale).astype(jnp.bfloat16)
    grad_query = jnp.dot(dscore, keys, preferred_element_type=jnp.float32).astype(jnp.bfloat16)
    grad_keys = outer_rows(dscore, query_rows).astype(jnp.bfloat16)
    grad_vals = outer_rows(weights, grad_rows).astype(jnp.bfloat16)
    tiles_grad = jnp.concatenate([grad_keys, grad_vals], axis=1).reshape(tiles.shape)
    sink_grad = -jnp.sum(sink_part / total * delta)
    return (attended, grad_query, tiles_grad, sink_grad)


def body(query, key, value, grad_out, chosen, placed, sink):
    seqs = query.shape[0]
    block = query.shape[3]
    width = DH
    hpd = query.shape[4] // width
    unit = key.shape[1]
    parts_per = block // unit
    n_ctx = lax.axis_size("ctx")
    nblk = n_ctx // parts_per
    place = lax.axis_index("ctx")
    slot = place // parts_per
    position = place % parts_per
    slots = jnp.arange(nblk, dtype=jnp.int32)
    seq_block = jnp.sum(jnp.where(slots == slot, placed, 0))
    slot_of = jnp.sum(jnp.where(placed[None, :] == slots[:, None], slots[None, :], 0), axis=1)
    mine = lax.dynamic_slice_in_dim(chosen, seq_block, 1, 1)[:, 0]
    mine = lax.dynamic_slice_in_dim(mine, position * hpd, hpd, 1)
    usable_pick = mine < seq_block
    mapped = jnp.sum(jnp.where(mine[..., None] == slots, slot_of, 0), axis=-1)
    mapped = jnp.where(usable_pick, mapped, slot)
    lead = jnp.broadcast_to(slot, mine.shape[:2] + (1,))
    picks = jnp.concatenate([lead, mapped], axis=-1)
    kinds = picks.shape[-1]
    usable = jnp.concatenate([jnp.ones(mine.shape[:2] + (1,), bool), usable_pick], axis=-1)
    sink_mine = lax.dynamic_slice_in_dim(sink, position * hpd, hpd)
    paired = jnp.concatenate(
        [
            key.reshape(seqs, unit, parts_per, hpd, width),
            value.reshape(seqs, unit, parts_per, hpd, width),
        ],
        axis=-1,
    )
    paired = jnp.transpose(paired, (2, 0, 3, 1, 4))
    items = seqs * hpd
    frag = unit * 2 * width // n_ctx
    seq_ix = jnp.arange(seqs, dtype=jnp.int32)[None, :, None, None, None]
    head_ix = jnp.arange(hpd, dtype=jnp.int32)[None, None, :, None, None]
    spread = jnp.transpose(paired.reshape(parts_per, seqs, hpd, n_ctx, frag), (3, 0, 1, 2, 4))
    held = lax.all_to_all(spread, "ctx", split_axis=0, concat_axis=0, tiled=True)
    held = jnp.transpose(held, (2, 3, 0, 1, 4)).reshape(seqs, hpd, n_ctx * parts_per, frag)
    match_block = placed[:, None] == slots[None, :]
    chosen_all = jnp.sum(jnp.where(match_block[None, :, :, None, None], chosen[:, None], 0), axis=2)
    before = chosen_all < placed[None, :, None, None]
    mapped_all = jnp.sum(jnp.where(chosen_all[..., None] == slots, slot_of, 0), axis=-1)
    own_slot = slots[None, :, None, None]
    mapped_all = jnp.where(before, mapped_all, own_slot)
    lead_all = jnp.broadcast_to(own_slot, mapped_all.shape[:3] + (1,))
    picks_all = jnp.concatenate([lead_all, mapped_all], axis=-1)
    picks_all = jnp.transpose(
        picks_all.reshape(seqs, nblk, parts_per, hpd, kinds), (1, 2, 0, 3, 4)
    ).reshape(n_ctx, seqs, hpd, kinds)
    dest_group = (jnp.arange(n_ctx, dtype=jnp.int32) % parts_per)[:, None, None, None, None]
    part_ids = jnp.arange(parts_per, dtype=jnp.int32)[None, None, None, None, :]
    route = (picks_all[..., None] * parts_per + part_ids) * parts_per + dest_group
    outgoing = held[seq_ix, head_ix, route]
    fetched = lax.all_to_all(outgoing, "ctx", split_axis=0, concat_axis=0, tiled=True)
    tiles_items = jnp.transpose(fetched, (1, 2, 3, 4, 0, 5)).reshape(
        items, kinds, parts_per * unit, 2 * width
    )
    query_heads = jnp.transpose(query.reshape(seqs, block, hpd, width), (0, 2, 1, 3)).reshape(
        items, block, width
    )
    grad_heads = jnp.transpose(grad_out.reshape(seqs, block, hpd, width), (0, 2, 1, 3)).reshape(
        items, block, width
    )
    sink_items = jnp.tile(sink_mine, seqs)

    def per_head(item):
        q_rows, g_rows, tiles, use_row, sink_logit = item
        return attend_block(q_rows, g_rows, tiles, use_row, sink_logit)

    atts, grads_q, tiles_grad, sink_grads = lax.map(
        per_head, (query_heads, grad_heads, tiles_items, usable.reshape(items, -1), sink_items)
    )
    attended = jnp.transpose(atts.reshape(seqs, hpd, block, width), (0, 2, 1, 3)).reshape(
        seqs, 1, 1, block, hpd * width
    )
    grad_query = jnp.transpose(grads_q.reshape(seqs, hpd, block, width), (0, 2, 1, 3)).reshape(
        seqs, 1, 1, block, hpd * width
    )
    shards = tiles_grad.reshape(seqs, hpd, kinds, parts_per, n_ctx, frag)
    sendback = jnp.transpose(shards, (4, 0, 1, 2, 3, 5))
    landed = lax.all_to_all(sendback, "ctx", split_axis=0, concat_axis=0, tiled=True)
    pooled = (
        jnp.zeros((seqs, hpd, n_ctx * parts_per, frag), jnp.float32)
        .at[seq_ix, head_ix, route]
        .add(landed.astype(jnp.float32))
    )
    pooled = jnp.transpose(pooled.reshape(seqs, hpd, n_ctx, parts_per, frag), (2, 3, 0, 1, 4))
    homed = lax.all_to_all(
        pooled.astype(jnp.bfloat16), "ctx", split_axis=0, concat_axis=0, tiled=True
    ).astype(pooled.dtype)
    totals = jnp.transpose(homed, (1, 2, 3, 0, 4)).reshape(parts_per, seqs, hpd, unit, 2 * width)
    totals = jnp.transpose(totals, (1, 3, 0, 2, 4))
    grad_key = totals[..., :width].reshape(seqs, unit, parts_per * hpd * width).astype(jnp.bfloat16)
    grad_value = (
        totals[..., width:].reshape(seqs, unit, parts_per * hpd * width).astype(jnp.bfloat16)
    )
    sink_local = jnp.sum(sink_grads.reshape(seqs, hpd), axis=0)
    start = lax.axis_index("head") * (parts_per * hpd) + position * hpd
    spread_sink = lax.dynamic_update_slice(jnp.zeros((HEADS,), jnp.float32), sink_local, (start,))
    grad_sink = lax.psum(spread_sink, ("dp", "ctx", "head"))
    return (attended, grad_query, grad_key, grad_value, grad_sink)


def solution(mesh):
    in_specs = (
        P("dp", "ctx", "head", None, None),
        P("dp", "ctx", "head"),
        P("dp", "ctx", "head"),
        P("dp", "ctx", "head", None, None),
        P("dp", None, "head", None),
        P(),
        P("head"),
    )
    out_specs = (
        P("dp", "ctx", "head", None, None),
        P("dp", "ctx", "head", None, None),
        P("dp", "ctx", "head"),
        P("dp", "ctx", "head"),
        P(),
    )
    return jax.shard_map(body, mesh=mesh, in_specs=in_specs, out_specs=out_specs, check_vma=False)
```

profile of v0, /device:TPU:1, one launch (start us, length us, event | category | flops | bytes accessed | tf_op | source)
XLA Modules:
  0.0 485.5 jit_solution(11513940544076405673)
XLA Ops:
  0.7 1.1 reshape.333
  1.8 1.1 reshape.334
  3.3 1.3 copy.152
  4.6 19.1 %all-to-all-start = ((bf16[64,4,1,2,512]{4,3,1,2,0:T(2,128)(2,1)}), bf16[64,4,1,2,512]{4,3,1,2,0:T(2,128)(2,1)S(1)}, u32[]{:S(2)}, u32[]{:S(2)}) async-start(bf16[64,4,1,2,512]{4,3,1,2,0:T(2,128)(2,1)} %copy.152), calls=%async_computation | async-start | bytes 1048576 | tf_op jit(solution)/shard_map/all_to_all | solution.py:92
  23.8 0.9 select_reduce_fusion.2
  24.8 1.0 select_reduce_fusion.1
  27.1 26.0 %all-to-all-done = bf16[64,4,1,2,512]{4,3,1,2,0:T(2,128)(2,1)S(1)} async-done(((bf16[64,4,1,2,512]{4,3,1,2,0:T(2,128)(2,1)}), bf16[64,4,1,2,512]{4,3,1,2,0:T(2,128)(2,1)S(1)}, u32[]{:S(2)}, u32[]{:S(2)}) %all-to-all-start) | async-done | bytes 524320 | tf_op jit(solution)/shard_map/all_to_all | solution.py:92
  53.2 14.1 %gather_fusion = bf16[2048,512]{1,0:T(8,128)(2,1)S(1)} fusion(bf16[1,2,256,512]{3,2,1,0:T(8,128)(2,1)S(1)} %copy.174, s32[2048]{0:T(1024)S(1)} %reshape.369), kind=kCustom, calls=%fused_computation | custom fusion | bytes 4218880 | tf_op jit(solution)/shard_map/gather | solution.py:108
  67.3 2.1 reshape.368
  69.4 9.0 %all-to-all-start.1 = ((bf16[64,1,2,4,4,512]{5,4,3,2,1,0:T(4,128)(2,1)}), bf16[64,1,2,4,4,512]{5,4,3,2,1,0:T(4,128)(2,1)S(1)}, u32[]{:S(2)}, u32[]{:S(2)}) async-start(bf16[64,1,2,4,4,512]{5,4,3,2,1,0:T(4,128)(2,1)} %bitcast.145), calls=%async_computation.1 | async-start | bytes 4194304 | tf_op jit(solution)/shard_map/all_to_all | solution.py:109
  82.3 86.9 %all-to-all-done.1 = bf16[64,1,2,4,4,512]{5,4,3,2,1,0:T(4,128)(2,1)S(1)} async-done(((bf16[64,1,2,4,4,512]{5,4,3,2,1,0:T(4,128)(2,1)}), bf16[64,1,2,4,4,512]{5,4,3,2,1,0:T(4,128)(2,1)S(1)}, u32[]{:S(2)}, u32[]{:S(2)}) %all-to-all-start.1) | async-done | bytes 2097184 | tf_op jit(solution)/shard_map/all_to_all | solution.py:109
  169.2 2.5 copy.159
  171.7 4.1 reshape.337
  175.8 54.9 %while.18 = (s32[]{:T(128)}, bf16[2,512,128]{2,1,0:T(8,128)(2,1)}, bf16[2,512,128]{2,1,0:T(8,128)(2,1)}, bf16[2,4,512,256]{3,2,1,0:T(8,128)(2,1)}, f32[2]{0:T(12...) while((s32[]{:T(128)}, bf16[2,512,128]{2,1,0:T(8,128)(2,1)}, ...), condition=%wide.region_9.10_spmd, body=%wide.region_4.9_spmd.sunk | while | flops 1629425152 | bytes 86695736 | solution.py:125
  176.5 2.6 select_reduce_fusion.5
  179.0 1.3 dynamic-slice_bitcast_fusion.2
  180.3 1.0 fusion.72
  181.4 2.4 fusion.76
  187.3 1.9 copy-done
  189.2 1.4 bitcast_dynamic-update-slice_fusion.2
  190.8 1.3 multiply_reduce_fusion.6
  192.9 3.3 multiply_convert_fusion.2
  197.2 1.3 copy.184
  198.5 2.3 constant_dynamic-update-slice_fusion.2
  200.8 2.4 fusion.80
  203.9 2.6 select_reduce_fusion.5
  206.5 1.3 dynamic-slice_bitcast_fusion.2
  207.8 1.0 fusion.72
  208.8 2.4 fusion.76
  214.7 1.9 copy-done
  216.6 1.4 bitcast_dynamic-update-slice_fusion.2
  218.3 1.3 multiply_reduce_fusion.6
  220.4 3.3 multiply_convert_fusion.2
  224.6 1.3 copy.184
  226.0 2.3 constant_dynamic-update-slice_fusion.2
  228.3 2.4 fusion.80
  230.7 2.7 reshape.344
  233.4 3.0 copy.167
  236.4 14.6 %all-to-all-start.2 = ((bf16[64,1,2,4,4,512]{5,4,3,2,1,0:T(4,128)(2,1)}), bf16[64,1,2,4,4,512]{5,4,3,2,1,0:T(4,128)(2,1)S(1)}, u32[]{:S(2)}, u32[]{:S(2)}) async-start(bf16[64,1,2,4,4,512]{5,4,3,2,1,0:T(4,128)(2,1)} %copy.167), calls=%async_computation.2 | async-start | bytes 4194304 | tf_op jit(solution)/shard_map/all_to_all | solution.py:136
  251.5 91.0 %all-to-all-done.2 = bf16[64,1,2,4,4,512]{5,4,3,2,1,0:T(4,128)(2,1)S(1)} async-done(((bf16[64,1,2,4,4,512]{5,4,3,2,1,0:T(4,128)(2,1)}), bf16[64,1,2,4,4,512]{5,4,3,2,1,0:T(4,128)(2,1)S(1)}, u32[]{:S(2)}, u32[]{:S(2)}) %all-to-all-start.2) | async-done | bytes 2097184 | tf_op jit(solution)/shard_map/all_to_all | solution.py:136
  342.5 2.5 reshape.379
  345.0 13.5 %scatter_custom_fusion = f32[512,512]{1,0:T(8,128)S(1)} fusion(s32[2048]{0:T(1024)S(1)} %reshape.377, f32[2048,512]{1,0:T(8,128)} %reshape.379, f32[]{:T(128)} %constant.166.clone.1), kind=kCustom, calls=%fused_computation.55 | custom fusion | flops 1048576 | bytes 1049088
  358.7 1.0 copy.168
  359.7 13.9 %all-to-all-start.3 = ((bf16[64,4,1,2,512]{4,1,3,2,0:T(4,128)(2,1)}), bf16[64,4,1,2,512]{4,1,3,2,0:T(4,128)(2,1)S(1)}, u32[]{:S(2)}, u32[]{:S(2)}) async-start(bf16[64,4,1,2,512]{4,1,3,2,0:T(4,128)(2,1)} %copy.168), calls=%async_computation.3 | async-start | bytes 1048576 | tf_op jit(solution)/shard_map/all_to_all | solution.py:143
  373.8 105.9 %psum.7 = f32[32]{0:T(128)} all-reduce(f32[32]{0:T(128)S(1)} %dynamic_update_slice.30), channel_id=1, replica_groups=mesh['dp'=2,'ctx'=64,'head'=4] {'dp','ctx','head'}, use_global_device_ids=true, to_apply=%region_11.12 | all-reduce | flops 32 | bytes 256 | tf_op jit(solution)/shard_map/psum | solution.py:155
  479.7 1.2 copy.163
  481.0 0.9 reshape.341
  482.1 0.9 reshape.343
  (118 shorter events, 18.5 us)
Async XLA Ops:
  0.6 25.9 %copy-start.10 = (s32[3]{0:T(128)S(1)}, s32[3]{0:T(128)}, u32[]{:S(2)}) copy-start(s32[3]{0:T(128)} %constant.189) | copy-start | bytes 40
  0.6 23.1 %copy-start.8 = (s32[16]{0:T(128)S(1)}, s32[16]{0:T(128)}, u32[]{:S(2)}) copy-start(s32[16]{0:T(128)} %param.14) | copy-start | bytes 196
  0.7 23.2 %copy-start.7 = (s32[1,16,8,3]{1,2,3,0:T(8,128)S(1)}, s32[1,16,8,3]{1,2,3,0:T(8,128)}, u32[]{:S(2)}) copy-start(s32[1,16,8,3]{1,2,3,0:T(8,128)} %param.13) | copy-start | bytes 4612
  4.6 48.5 %all-to-all-start = ((bf16[64,4,1,2,512]{4,3,1,2,0:T(2,128)(2,1)}), bf16[64,4,1,2,512]{4,3,1,2,0:T(2,128)(2,1)S(1)}, u32[]{:S(2)}, u32[]{:S(2)}) async-start(bf16[64,4,1,2,512]{4,3,1,2,0:T(2,128)(2,1)} %copy.152), calls=%async_computation | async-start | bytes 1048576 | tf_op jit(solution)/shard_map/all_to_all | solution.py:92
  67.3 13.9 %copy-start.11 = (f32[8]{0:T(128)S(1)}, f32[8]{0:T(128)}, u32[]{:S(2)}) copy-start(f32[8]{0:T(128)} %param.15) | copy-start | bytes 100
  67.3 14.0 %copy-start.4 = (bf16[1,1,1,512,256]{4,3,2,1,0:T(8,128)(2,1)S(1)}, bf16[1,1,1,512,256]{4,3,2,1,0:T(8,128)(2,1)}, u32[]{:S(2)}) copy-start(bf16[1,1,1,512,256]{4,3,2,1,0:T(8,128)(2,1)} %param.9) | copy-start | bytes 786436
  69.4 12.0 %copy-start.5 = (bf16[1,1,1,512,256]{4,3,2,1,0:T(8,128)(2,1)S(1)}, bf16[1,1,1,512,256]{4,3,2,1,0:T(8,128)(2,1)}, u32[]{:S(2)}) copy-start(bf16[1,1,1,512,256]{4,3,2,1,0:T(8,128)(2,1)} %param.12) | copy-start | bytes 786436
  69.4 99.8 %all-to-all-start.1 = ((bf16[64,1,2,4,4,512]{5,4,3,2,1,0:T(4,128)(2,1)}), bf16[64,1,2,4,4,512]{5,4,3,2,1,0:T(4,128)(2,1)S(1)}, u32[]{:S(2)}, u32[]{:S(2)}) async-start(bf16[64,1,2,4,4,512]{5,4,3,2,1,0:T(4,128)(2,1)} %bitcast.145), calls=%async_computation.1 | async-start | bytes 4194304 | tf_op jit(solution)/shard_map/all_to_all | solution.py:109
  175.8 14.8 %copy-start.2 = (bf16[2,512,128]{1,2,0:T(8,128)(2,1)}, bf16[2,512,128]{1,2,0:T(8,128)(2,1)S(1)}, u32[]{:S(2)}) copy-start(bf16[2,512,128]{1,2,0:T(8,128)(2,1)S(1)} %get-tuple-element.386) | copy-start | bytes 786436 | tf_op jit(solution)/shard_map/while
  187.2 1.9 copy-start
  192.9 3.7 copy-start.1
  198.5 4.7 copy-start.3
  203.2 14.8 %copy-start.2 = (bf16[2,512,128]{1,2,0:T(8,128)(2,1)}, bf16[2,512,128]{1,2,0:T(8,128)(2,1)S(1)}, u32[]{:S(2)}) copy-start(bf16[2,512,128]{1,2,0:T(8,128)(2,1)S(1)} %get-tuple-element.386) | copy-start | bytes 786436 | tf_op jit(solution)/shard_map/while
  214.7 1.9 copy-start
  220.4 3.7 copy-start.1
  226.0 4.7 copy-start.3
  233.4 17.6 %copy-start.9 = (s32[3]{0:T(128)S(1)}, s32[3]{0:T(128)}, u32[]{:S(2)}) copy-start(s32[3]{0:T(128)} %constant.192) | copy-start | bytes 40
  236.4 106.2 %all-to-all-start.2 = ((bf16[64,1,2,4,4,512]{5,4,3,2,1,0:T(4,128)(2,1)}), bf16[64,1,2,4,4,512]{5,4,3,2,1,0:T(4,128)(2,1)S(1)}, u32[]{:S(2)}, u32[]{:S(2)}) async-start(bf16[64,1,2,4,4,512]{5,4,3,2,1,0:T(4,128)(2,1)} %copy.167), calls=%async_computation.2 | async-start | bytes 4194304 | tf_op jit(solution)/shard_map/all_to_all | solution.py:136
  345.0 136.8 %copy-start.6 = (bf16[2,512,128]{2,1,0:T(8,128)(2,1)S(1)}, bf16[2,512,128]{2,1,0:T(8,128)(2,1)}, u32[]{:S(2)}) copy-start(bf16[2,512,128]{2,1,0:T(8,128)(2,1)} %get-tuple-element.137) | copy-start | bytes 786436
  359.7 123.3 %all-to-all-start.3 = ((bf16[64,4,1,2,512]{4,1,3,2,0:T(4,128)(2,1)}), bf16[64,4,1,2,512]{4,1,3,2,0:T(4,128)(2,1)S(1)}, u32[]{:S(2)}, u32[]{:S(2)}) async-start(bf16[64,4,1,2,512]{4,1,3,2,0:T(4,128)(2,1)} %copy.168), calls=%async_computation.3 | async-start | bytes 1048576 | tf_op jit(solution)/shard_map/all_to_all | solution.py:143
where the time goes:
time: 487 us; the launch traced here: 486 us
  waiting for transfers between devices  204 us (42%)
  blocking collectives  106 us (22%)
  local copies, waits for them, and re-layouts  62.7 us (13%)
  starting transfers between devices  56.5 us (12%)
  other arithmetic  31.3 us (6%)
  matrix products  20.7 us (4%)
    psum x1, blocking collectives, body(): grad_sink = lax.psum(spread_sink, ('dp', 'ctx', 'head'))  106 us
    all_to_all x1, waiting for transfers between devices, body(): lax.all_to_all(sendback, 'ctx', split_axis=0, concat_axis=0, tiled=True)  91 us
    all_to_all x1, waiting for transfers between devices, body(): lax.all_to_all(outgoing, 'ctx', split_axis=0, concat_axis=0, tiled=True)  86.9 us
    all_to_all x1, waiting for transfers between devices, body(): lax.all_to_all(spread, 'ctx', split_axis=0, concat_axis=0, tiled=True)  26 us
    all_to_all x1, starting transfers between devices, body(): lax.all_to_all(spread, 'ctx', split_axis=0, concat_axis=0, tiled=True)  19.1 us
    gather x2, local copies, waits for them, and re-layouts, body(): outgoing = held[seq_ix, head_ix, route]  16.2 us
    all_to_all x1, starting transfers between devices, body(): lax.all_to_all(sendback, 'ctx', split_axis=0, concat_axis=0, tiled=True)  14.6 us
    all_to_all x1, starting transfers between devices, body(): lax.all_to_all(pooled.astype(jnp.bfloat16), 'ctx', split_axis=0, concat_a...  13.9 us
  transfers between devices with their start and end apart: 4, of which 3 were waited for; matrix products, arithmetic and copies ran while one was open for 2% of the time, Pallas kernels for 0%

commit v1 on v0

--- a/solution.py
+++ b/solution.py
@@ -152,7 +152,8 @@
     sink_local = jnp.sum(sink_grads.reshape(seqs, hpd), axis=0)
     start = lax.axis_index("head") * (parts_per * hpd) + position * hpd
     spread_sink = lax.dynamic_update_slice(jnp.zeros((HEADS,), jnp.float32), sink_local, (start,))
-    grad_sink = lax.psum(spread_sink, ("dp", "ctx", "head"))
+    z1 = jax.lax.all_gather(spread_sink, axis_name=("dp", "ctx", "head"))
+    grad_sink = jnp.sum(z1, 0)
     return (attended, grad_query, grad_key, grad_value, grad_sink)
 
 

time: 487 us -> 1630 us (3.35)
  blocking collectives: 106 us -> 1250 us
    all_gather x0 -> x1, blocking collectives: none -> 1250 us  [body(): z1 = jax.lax.all_gather(spread_sink, axis_name=('dp', 'ctx', 'head'))]
    psum x1 -> x0, blocking collectives: 106 us -> none  [body(): grad_sink = lax.psum(spread_sink, ('dp', 'ctx', 'head'))]
  transfers between devices with their start and end apart: 4 -> 4, of which waited for: 3 -> 3; matrix products, arithmetic and copies ran while one was open for 2% -> 1% of each run, Pallas kernels for 0% -> 0%
where the time goes in v1:
time: 1630 us
  blocking collectives  1250 us (77%)
  waiting for transfers between devices  204 us (13%)
  local copies, waits for them, and re-layouts  62.6 us (4%)
  starting transfers between devices  56.5 us (3%)
  other arithmetic  32.4 us (2%)
  matrix products  20.7 us (1%)
    all_gather x1, blocking collectives, body(): z1 = jax.lax.all_gather(spread_sink, axis_name=('dp', 'ctx', 'head'))  1250 us
    all_to_all x1, waiting for transfers between devices, body(): lax.all_to_all(sendback, 'ctx', split_axis=0, concat_axis=0, tiled=True)  91 us
    all_to_all x1, waiting for transfers between devices, body(): lax.all_to_all(outgoing, 'ctx', split_axis=0, concat_axis=0, tiled=True)  86.9 us
  transfers between devices with their start and end apart: 4, of which 3 were waited for; matrix products, arithmetic and copies ran while one was open for 1% of the time, Pallas kernels for 0%

profile of v1, /device:TPU:1, one launch (start us, length us, event | category | flops | bytes accessed | tf_op | source)
XLA Modules:
  0.0 1627.4 jit_solution(2943128888998168485)
XLA Ops:
  0.7 1.1 reshape.336
  1.8 1.1 reshape.337
  3.3 1.3 copy.152
  4.6 19.1 %all-to-all-start = ((bf16[64,4,1,2,512]{4,3,1,2,0:T(2,128)(2,1)}), bf16[64,4,1,2,512]{4,3,1,2,0:T(2,128)(2,1)S(1)}, u32[]{:S(2)}, u32[]{:S(2)}) async-start(bf16[64,4,1,2,512]{4,3,1,2,0:T(2,128)(2,1)} %copy.152), calls=%async_computation | async-start | bytes 1048576 | tf_op jit(solution)/shard_map/all_to_all | solution.py:92
  23.8 0.9 select_reduce_fusion.2
  24.8 1.0 select_reduce_fusion.1
  27.1 26.0 %all-to-all-done = bf16[64,4,1,2,512]{4,3,1,2,0:T(2,128)(2,1)S(1)} async-done(((bf16[64,4,1,2,512]{4,3,1,2,0:T(2,128)(2,1)}), bf16[64,4,1,2,512]{4,3,1,2,0:T(2,128)(2,1)S(1)}, u32[]{:S(2)}, u32[]{:S(2)}) %all-to-all-start) | async-done | bytes 524320 | tf_op jit(solution)/shard_map/all_to_all | solution.py:92
  53.2 14.1 gather_fusion
  67.3 2.1 reshape.371
  69.4 9.0 all-to-all-start.1
  82.3 86.9 %all-to-all-done.1 = bf16[64,1,2,4,4,512]{5,4,3,2,1,0:T(4,128)(2,1)S(1)} async-done(((bf16[64,1,2,4,4,512]{5,4,3,2,1,0:T(4,128)(2,1)}), bf16[64,1,2,4,4,512]{5,4,3,2,1,0:T(4,128)(2,1)S(1)}, u32[]{:S(2)}, u32[]{:S(2)}) %all-to-all-start.1) | async-done | bytes 2097184 | tf_op jit(solution)/shard_map/all_to_all | solution.py:109
  169.2 2.5 copy.159
  171.7 4.1 reshape.340
  175.8 54.9 %while.18 = (s32[]{:T(128)}, bf16[2,512,128]{2,1,0:T(8,128)(2,1)}, bf16[2,512,128]{2,1,0:T(8,128)(2,1)}, bf16[2,4,512,256]{3,2,1,0:T(8,128)(2,1)}, f32[2]{0:T(12...) while((s32[]{:T(128)}, bf16[2,512,128]{2,1,0:T(8,128)(2,1)}, ...), condition=%wide.region_9.10_spmd, body=%wide.region_4.9_spmd.sunk | while | flops 1629425152 | bytes 86695736 | solution.py:125
  176.5 2.6 select_reduce_fusion.5
  179.0 1.3 dynamic-slice_bitcast_fusion.2
  180.3 1.0 fusion.72
  181.4 2.4 fusion.76
  187.3 1.9 copy-done
  189.2 1.4 bitcast_dynamic-update-slice_fusion.2
  190.8 1.3 multiply_reduce_fusion.6
  192.9 3.3 multiply_convert_fusion.2
  197.2 1.3 copy.184
  198.5 2.3 constant_dynamic-update-slice_fusion.2
  200.8 2.4 fusion.80
  203.9 2.6 select_reduce_fusion.5
  206.5 1.3 dynamic-slice_bitcast_fusion.2
  207.8 1.0 fusion.72
  208.8 2.4 fusion.76
  214.7 1.9 copy-done
  216.6 1.4 bitcast_dynamic-update-slice_fusion.2
  218.3 1.3 multiply_reduce_fusion.6
  220.4 3.3 multiply_convert_fusion.2
  224.6 1.3 copy.184
  226.0 2.3 constant_dynamic-update-slice_fusion.2
  228.3 2.4 fusion.80
  230.7 2.7 reshape.347
  233.4 3.0 copy.167
  236.4 14.6 all-to-all-start.2
  251.5 91.0 %all-to-all-done.2 = bf16[64,1,2,4,4,512]{5,4,3,2,1,0:T(4,128)(2,1)S(1)} async-done(((bf16[64,1,2,4,4,512]{5,4,3,2,1,0:T(4,128)(2,1)}), bf16[64,1,2,4,4,512]{5,4,3,2,1,0:T(4,128)(2,1)S(1)}, u32[]{:S(2)}, u32[]{:S(2)}) %all-to-all-start.2) | async-done | bytes 2097184 | tf_op jit(solution)/shard_map/all_to_all | solution.py:136
  342.5 2.5 reshape.382
  345.0 13.5 scatter_custom_fusion
  358.7 1.0 copy.168
  359.7 13.9 all-to-all-start.3
  373.6 1.2 copy.163
  374.8 0.9 reshape.344
  376.9 1246.9 %all-gather = f32[512,1,32]{2,1,0:T(1,128)S(1)} all-gather(f32[1,1,32]{2,1,0:T(1,128)S(1)} %dynamic_update_slice.32), channel_id=1, replica_groups=mesh['dp'=2,'ctx'=64,'head'=4] {'dp','ctx','head'}, dimensions={0}, use_global_device_ids=true | all-gather | bytes 65664 | tf_op jit(solution)/shard_map/all_gather | solution.py:155
  1623.8 1.1 reduce_sum.95
  (119 shorter events, 19.2 us)
Async XLA Ops:
  0.6 25.9 %copy-start.10 = (s32[3]{0:T(128)S(1)}, s32[3]{0:T(128)}, u32[]{:S(2)}) copy-start(s32[3]{0:T(128)} %constant.190) | copy-start | bytes 40
  0.6 23.1 %copy-start.8 = (s32[16]{0:T(128)S(1)}, s32[16]{0:T(128)}, u32[]{:S(2)}) copy-start(s32[16]{0:T(128)} %param.14) | copy-start | bytes 196
  0.7 23.2 %copy-start.7 = (s32[1,16,8,3]{1,2,3,0:T(8,128)S(1)}, s32[1,16,8,3]{1,2,3,0:T(8,128)}, u32[]{:S(2)}) copy-start(s32[1,16,8,3]{1,2,3,0:T(8,128)} %param.13) | copy-start | bytes 4612
  4.6 48.5 %all-to-all-start = ((bf16[64,4,1,2,512]{4,3,1,2,0:T(2,128)(2,1)}), bf16[64,4,1,2,512]{4,3,1,2,0:T(2,128)(2,1)S(1)}, u32[]{:S(2)}, u32[]{:S(2)}) async-start(bf16[64,4,1,2,512]{4,3,1,2,0:T(2,128)(2,1)} %copy.152), calls=%async_computation | async-start | bytes 1048576 | tf_op jit(solution)/shard_map/all_to_all | solution.py:92
  67.3 13.9 copy-start.11
  67.3 14.0 copy-start.4
  69.4 12.0 copy-start.5
  69.4 99.8 %all-to-all-start.1 = ((bf16[64,1,2,4,4,512]{5,4,3,2,1,0:T(4,128)(2,1)}), bf16[64,1,2,4,4,512]{5,4,3,2,1,0:T(4,128)(2,1)S(1)}, u32[]{:S(2)}, u32[]{:S(2)}) async-start(bf16[64,1,2,4,4,512]{5,4,3,2,1,0:T(4,128)(2,1)} %bitcast.146), calls=%async_computation.1 | async-start | bytes 4194304 | tf_op jit(solution)/shard_map/all_to_all | solution.py:109
  175.8 14.8 copy-start.2
  187.2 1.9 copy-start
  192.9 3.7 copy-start.1
  198.5 4.7 copy-start.3
  203.2 14.8 copy-start.2
  214.7 1.9 copy-start
  220.4 3.7 copy-start.1
  226.0 4.7 copy-start.3
  233.4 17.6 %copy-start.9 = (s32[3]{0:T(128)S(1)}, s32[3]{0:T(128)}, u32[]{:S(2)}) copy-start(s32[3]{0:T(128)} %constant.193) | copy-start | bytes 40
  236.4 106.2 %all-to-all-start.2 = ((bf16[64,1,2,4,4,512]{5,4,3,2,1,0:T(4,128)(2,1)}), bf16[64,1,2,4,4,512]{5,4,3,2,1,0:T(4,128)(2,1)S(1)}, u32[]{:S(2)}, u32[]{:S(2)}) async-start(bf16[64,1,2,4,4,512]{5,4,3,2,1,0:T(4,128)(2,1)} %copy.167), calls=%async_computation.2 | async-start | bytes 4194304 | tf_op jit(solution)/shard_map/all_to_all | solution.py:136
  345.0 30.7 %copy-start.6 = (bf16[2,512,128]{2,1,0:T(8,128)(2,1)S(1)}, bf16[2,512,128]{2,1,0:T(8,128)(2,1)}, u32[]{:S(2)}) copy-start(bf16[2,512,128]{2,1,0:T(8,128)(2,1)} %get-tuple-element.137) | copy-start | bytes 786436
  359.7 1265.1 %all-to-all-start.3 = ((bf16[64,4,1,2,512]{4,1,3,2,0:T(4,128)(2,1)}), bf16[64,4,1,2,512]{4,1,3,2,0:T(4,128)(2,1)S(1)}, u32[]{:S(2)}, u32[]{:S(2)}) async-start(bf16[64,4,1,2,512]{4,1,3,2,0:T(4,128)(2,1)} %copy.168), calls=%async_computation.3 | async-start | bytes 1048576 | tf_op jit(solution)/shard_map/all_to_all | solution.py:143
